TPU v7x, 32 devices: a whole 2x2x4 slice. The times are simulated.
32 devices in a mesh: group: 2 (over y), dev: 8 (over z, x), tp: 2 (over core).
Axes of the slice: x: 2, y: 2, z: 4, core: 2. Of those that a mesh axis runs over, the one named last changes fastest.
Arguments:
- prompt_activations: bfloat16 [4096, 8192], P(('group', 'dev')), parts along dimension 0, may hold values from -6 to 6
- key_matrix: bfloat16 [8192, 512], P('dev', 'tp'), may hold values from -0.0625 to 0.0625
- value_matrix: bfloat16 [8192, 512], P('dev', 'tp'), may hold values from -0.0625 to 0.0625
- adapter_down_keyvalue: bfloat16 [8192, 128], P('dev'), may hold values from -0.0625 to 0.0625
- adapter_up_key: bfloat16 [64, 512], P(None, 'tp'), may hold values from -1.5 to 1.5
- adapter_up_value: bfloat16 [64, 512], P(None, 'tp'), may hold values from -1.5 to 1.5
- request_adapter: int32 [16], P('group'), parts along dimension 0, may hold values from 0 to 3
- page_request: int32 [1024, 1], P('group'), parts along dimension 0, may hold values from 0 to 7; in each aligned block of 64 rows (0 to 63, 64 to 127, ...) at most 8 rows name the same one
- context_tokens: int32 [16], P('group'), parts along dimension 0, may hold values from 64 to 256
- step_query: bfloat16 [16, 4096], P(('group', 'dev'), 'tp'), parts along dimension 0, may hold values from -256 to 256
- step_key: bfloat16 [16, 512], P(('group', 'dev'), 'tp'), parts along dimension 0, may hold values from -6 to 6
- step_value: bfloat16 [16, 512], P(('group', 'dev'), 'tp'), parts along dimension 0, may hold values from -6 to 6
- stored_keys: bfloat16 [16, 256, 512], P(('group', 'dev'), None, 'tp'), parts along dimension 0, may hold values from -6 to 6
- stored_values: bfloat16 [16, 256, 512], P(('group', 'dev'), None, 'tp'), parts along dimension 0, may hold values from -6 to 6
- output_matrix: bfloat16 [4096, 8192], P('tp', 'dev'), may hold values from -0.09375 to 0.09375
- adapter_down_output: bfloat16 [4096, 64], P('tp'), may hold values from -0.09375 to 0.09375
- adapter_up_output: bfloat16 [64, 8192], P(None, 'dev'), may hold values from -1.5 to 1.5
Outputs:
- attended: bfloat16 [16, 8192], P('group', 'dev'), parts along dimension 0
There are 2 independent parts, one for each index of `group`. A program takes and returns all parts, laid end to end along the dimension named above; an argument that names none is the same for every part. Nothing has to cross between parts.
Inputs may be any that keep to these rules, and one draw needn't show every extreme that they name: `page_request`: among the pages of one device's prompt block (aligned blocks of 64 pages), no request owns more than 8; every request owns at least one page.
All inputs are finite; a program needn't handle non-finite values.
Results may differ from a plain program's by a relative error of at most 0.0086.
Values may be sent and summed in bfloat16 or wider, within the bound.
A program may use at most 64 MiB of HBM per device.

v0:
```python
import jax
import jax.numpy as jnp
from jax import lax
from jax.sharding import PartitionSpec as P

HEADS = 32
KV_HEADS = 4
HEAD = 128
LOW_RANK = 16
ADAPTER_COUNT = 4
PAGE = 4


adapter_scale = 1.0
rope_base = 500000.0


def rotate(key_rows, positions):
    row_count = key_rows.shape[0]
    blocks = key_rows.reshape(row_count, -1, HEAD)
    half_size = HEAD // 2
    exponent = jnp.arange(half_size, dtype=jnp.float32) * (2.0 / HEAD)
    frequency = jnp.exp(-jnp.log(jnp.float32(rope_base)) * exponent)
    angles = positions.astype(jnp.float32)[:, None] * frequency[None, :]
    cosine = jnp.cos(angles)[:, None, :]
    sine_part = jnp.sin(angles)[:, None, :]
    first_half = blocks[..., :half_size]
    second_half = blocks[..., half_size:]
    turned = jnp.concatenate(
        [
            first_half * cosine - second_half * sine_part,
            second_half * cosine + first_half * sine_part,
        ],
        axis=-1,
    )
    return turned.reshape(row_count, -1)


def owner_ranks(owners, row_total):
    onehot = (owners[:, None] == jnp.arange(row_total, dtype=jnp.int32)[None, :]).astype(jnp.int32)
    before = jnp.cumsum(onehot, axis=0) - onehot
    rank = jnp.sum(before * onehot, axis=1)
    return (onehot, rank)


def mask_columns(narrowed, adapter_list):
    column = jnp.arange(narrowed.shape[1], dtype=jnp.int32)
    owner = column % (ADAPTER_COUNT * LOW_RANK) // LOW_RANK
    return jnp.where(owner[None, :] == adapter_list[:, None], narrowed, jnp.zeros_like(narrowed))


def selected_narrow(activation_rows, adapter_down, adapter_list):
    narrowed = jnp.dot(activation_rows, adapter_down, preferred_element_type=jnp.float32)
    return mask_columns(narrowed, adapter_list)


def widened(selected_rows, up_key, up_value):
    split_at = ADAPTER_COUNT * LOW_RANK
    highest = lax.Precision.HIGHEST
    key_portion = jnp.dot(
        selected_rows[:, :split_at], up_key.astype(jnp.float32), precision=highest
    )
    value_portion = jnp.dot(
        selected_rows[:, split_at:], up_value.astype(jnp.float32), precision=highest
    )
    return (adapter_scale * key_portion, adapter_scale * value_portion)


def attend_local(
    query,
    old_keys,
    old_values,
    old_length,
    fresh_keys,
    fresh_values,
    fresh_valid,
    last_key,
    last_value,
):
    group_size = HEADS // KV_HEADS
    query_heads = query.reshape(-1, group_size, HEAD)
    kv_local = query_heads.shape[0]
    scale_factor = HEAD ** (-0.5)

    def score_of(key_rows):
        shaped = key_rows.reshape(key_rows.shape[0], kv_local, HEAD)
        return (
            jnp.einsum("kgd,lkd->kgl", query_heads, shaped, preferred_element_type=jnp.float32)
            * scale_factor
        )

    def mix_with(probs, value_rows):
        shaped = value_rows.reshape(value_rows.shape[0], kv_local, HEAD)
        return jnp.einsum("kgl,lkd->kgd", probs, shaped, preferred_element_type=jnp.float32)

    old_valid = jnp.arange(old_keys.shape[0], dtype=jnp.int32) < old_length
    old_scores = jnp.where(old_valid[None, None, :], score_of(old_keys), -1e30)
    fresh_scores = jnp.where(fresh_valid[None, None, :], score_of(fresh_keys), -1e30)
    last_score = score_of(last_key[None, :])
    top = jnp.maximum(
        jnp.maximum(
            jnp.max(old_scores, axis=-1, keepdims=True),
            jnp.max(fresh_scores, axis=-1, keepdims=True),
        ),
        last_score,
    )
    old_weights = jnp.exp(old_scores - top)
    fresh_weights = jnp.exp(fresh_scores - top)
    last_weight = jnp.exp(last_score - top)
    total = (
        jnp.sum(old_weights, axis=-1, keepdims=True)
        + jnp.sum(fresh_weights, axis=-1, keepdims=True)
        + last_weight
    )
    output = mix_with((old_weights / total).astype(jnp.bfloat16), old_values)
    output = output + mix_with((fresh_weights / total).astype(jnp.bfloat16), fresh_values)
    output = output + mix_with((last_weight / total).astype(jnp.bfloat16), last_value[None, :])
    return output.reshape(-1).astype(jnp.bfloat16)


def per_device(
    prompt_activations,
    key_matrix,
    value_matrix,
    adapter_down_keyvalue,
    adapter_up_key,
    adapter_up_value,
    request_adapter,
    page_request,
    context_tokens,
    step_query,
    step_key,
    step_value,
    stored_keys,
    stored_values,
    output_matrix,
    adapter_down_output,
    adapter_up_output,
):
    devices = lax.axis_size("dev")
    device = lax.axis_index("dev")
    tok_count = prompt_activations.shape[0]
    pages_here = tok_count // PAGE
    capacity = max(2, (pages_here + devices - 1) // devices)
    row_total = request_adapter.shape[0]
    owners = page_request[:, 0]
    onehot, rank = owner_ranks(owners, row_total)
    first_page = device * pages_here
    my_owners = lax.dynamic_slice_in_dim(owners, first_page, pages_here, 0)
    my_rank = lax.dynamic_slice_in_dim(rank, first_page, pages_here, 0)
    tokens = jnp.arange(tok_count, dtype=jnp.int32)
    token_page = tokens // PAGE
    token_owner = jnp.take(my_owners, token_page)
    position = (
        jnp.take(context_tokens, token_owner) + jnp.take(my_rank, token_page) * PAGE + tokens % PAGE
    )
    adapter_list = jnp.take(request_adapter, token_owner)
    key_width = key_matrix.shape[1]

    def add_rows(portion):
        return jnp.dot(prompt_activations, portion, preferred_element_type=jnp.float32)

    key_raw = add_rows(lax.all_gather(key_matrix, "dev", axis=0, tiled=True))
    value_raw = add_rows(lax.all_gather(value_matrix, "dev", axis=0, tiled=True))
    down_complete = lax.all_gather(adapter_down_keyvalue, "dev", axis=0, tiled=True)
    narrowed = jnp.dot(prompt_activations, down_complete, preferred_element_type=jnp.float32)
    selected_rows = mask_columns(narrowed, adapter_list)
    key_delta, value_delta = widened(selected_rows, adapter_up_key, adapter_up_value)
    key_rows = rotate(key_raw + key_delta, position).astype(jnp.bfloat16)
    value_rows = (value_raw + value_delta).astype(jnp.bfloat16)
    joined_rows = jnp.concatenate([key_rows, value_rows], axis=1)
    local_hot = (my_owners[:, None] == jnp.arange(row_total, dtype=jnp.int32)[None, :]).astype(
        jnp.int32
    )
    local_before = jnp.cumsum(local_hot, axis=0) - local_hot
    local_slot = jnp.sum(local_before * local_hot, axis=1)
    peer_slots = capacity * PAGE
    target = token_owner * peer_slots + jnp.take(local_slot, token_page) * PAGE + tokens % PAGE
    outgoing = (
        jnp.zeros((devices * peer_slots, 2 * key_width), jnp.bfloat16).at[target].set(joined_rows)
    )
    outgoing = outgoing.reshape(devices, peer_slots, 2 * key_width)
    incoming = lax.all_to_all(outgoing, "dev", split_axis=0, concat_axis=0, tiled=True)
    fresh_keys = incoming[:, :, :key_width].reshape(-1, key_width)
    fresh_values = incoming[:, :, key_width:].reshape(-1, key_width)
    my_column = jnp.take(onehot, device, axis=1)
    count_from = jnp.sum(my_column.reshape(devices, pages_here), axis=1)
    slot_page = jnp.arange(peer_slots, dtype=jnp.int32) // PAGE
    fresh_valid = (slot_page[None, :] < count_from[:, None]).reshape(-1)
    mixed_local = attend_local(
        step_query[0],
        stored_keys[0],
        stored_values[0],
        jnp.take(context_tokens, device),
        fresh_keys,
        fresh_values,
        fresh_valid,
        step_key[0],
        step_value[0],
    ).reshape(1, -1)
    portion = lax.all_gather(mixed_local, "dev", axis=0, tiled=True)
    plain_result = jnp.dot(portion, output_matrix, preferred_element_type=jnp.float32)
    selected_output = selected_narrow(portion, adapter_down_output, request_adapter)
    partial_output = plain_result + adapter_scale * jnp.dot(
        selected_output, adapter_up_output.astype(jnp.float32), precision=lax.Precision.HIGHEST
    )
    return lax.psum(partial_output, "tp").astype(jnp.bfloat16)


def solution(mesh):
    return jax.shard_map(
        per_device,
        mesh=mesh,
        in_specs=(
            P(("group", "dev"), None),
            P("dev", "tp"),
            P("dev", "tp"),
            P("dev", None),
            P(None, "tp"),
            P(None, "tp"),
            P("group"),
            P("group", None),
            P("group"),
            P(("group", "dev"), "tp"),
            P(("group", "dev"), "tp"),
            P(("group", "dev"), "tp"),
            P(("group", "dev"), None, "tp"),
            P(("group", "dev"), None, "tp"),
            P("tp", "dev"),
            P("tp", None),
            P(None, "dev"),
        ),
        out_specs=P("group", "dev"),
        check_vma=False,
    )
```

profile of v0, /device:TPU:0, one launch (start us, length us, event | category | flops | bytes accessed | tf_op | source)
XLA Modules:
  0.0 273.4 jit_solution(10275499087581960177)
XLA Ops:
  6.5 0.7 all-gather.7.cloned.1.call-update
  7.3 0.7 all-gather.9.cloned.1.call-update
  8.0 0.0 all-gather.5.cloned.1.call-start
  8.1 0.7 all-gather.5.cloned.1.call-update
  8.8 0.7 fusion.22
  9.4 1.1 reduce-window.6
  10.6 0.2 slice_reduce_fusion
  10.8 0.8 fusion.20
  11.6 0.1 dynamic_slice.10
  11.7 0.7 dynamic-slice_bitcast_fusion
  12.4 1.9 gather_fusion
  14.3 1.9 gather_fusion.2
  16.2 0.7 fusion.21
  16.9 0.1 select_n.127
  17.0 0.1 reduce_sum.45
  17.1 0.1 fusion.18
  17.2 0.1 reduce_window_sum.26
  17.3 0.2 select_reduce_fusion
  17.4 1.9 gather_fusion.1
  19.3 0.7 fusion.46
  20.6 0.7 fusion.47
  21.3 0.1 broadcast_compare_fusion
  21.4 9.7 %fusion.41 = (f32[256]{0:T(256)S(1)}, s32[256]{0:T(256)S(1)}, s32[256]{0:T(256)S(1)}) fusion(s32[256]{0:T(256)S(1)} %gather_fusion.2, s32[]{:T(128)} %bitcast.19, s32[]{:T(128)} %bitcast.18, s32[]{:T(128)} %bitcast.17, s32[]{:T(128)} %bitcast.16, s32[]{:T(128)} %bitcast.15, s32[]{:T(128)} %bitcast.14, s32[]{:T(128)} %bitcast.13, s32[]{:T(128)} %bitcast.12, ...), kind=kLoop, calls=%fused_computation.94 | loop fusion | flops 15616 | bytes 6208 | tf_op jit(solution)/shard_map/convert_element_type | solution.py:24
  31.1 0.3 multiply_cosine_fusion
  31.4 29.8 %all-gather.7.cloned.1.call-done = bf16[8192,128]{1,0:T(8,128)(2,1)} async-done(((bf16[1024,128]{1,0:T(8,128)(2,1)}), bf16[8192,128]{1,0:T(8,128)(2,1)}) %all-gather.7.cloned.1.call-update) | async-done | bytes 2097168 | tf_op jit(solution)/shard_map/all_gather | solution.py:165
  61.3 4.4 %convolution_select_fusion = f32[256,128]{0,1:T(8,128)S(1)} fusion(bf16[256,8192]{1,0:T(8,128)(2,1)} %param.21, bf16[8192,128]{1,0:T(8,128)(2,1)} %all-gather.7.cloned.1.call-done, s32[256]{0:T(256)S(1)} %get-tuple-element.40, s32[128]{0:T(128)S(1)} %and_select_fusion.2), kind=kOutput, calls=%fused_computation.7 | convolution fusion | flops 536936448 | bytes 6424064 | tf_op jit(solution)/shard_map/dot_general | solution.py:166
  65.6 69.1 %all-gather.9.cloned.1.call-done = bf16[8192,256]{1,0:T(8,128)(2,1)} async-done(((bf16[1024,256]{1,0:T(8,128)(2,1)}), bf16[8192,256]{1,0:T(8,128)(2,1)}) %all-gather.9.cloned.1.call-update) | async-done | bytes 4194320 | tf_op jit(solution)/shard_map/all_gather | solution.py:164
  134.7 5.2 %fusion.51 = f32[256,256]{0,1:T(8,128)S(1)} fusion(bf16[256,8192]{1,0:T(8,128)(2,1)} %param.21, bf16[8192,256]{1,0:T(8,128)(2,1)} %all-gather.9.cloned.1.call-done), kind=kOutput, calls=%fused_computation.123 | convolution fusion | flops 1073741824 | bytes 8650752 | tf_op jit(solution)/shard_map/dot_general | solution.py:161
  139.9 0.3 fusion
  140.3 67.9 %all-gather.5.cloned.1.call-done = bf16[8192,256]{1,0:T(8,128)(2,1)} async-done(((bf16[1024,256]{1,0:T(8,128)(2,1)}), bf16[8192,256]{1,0:T(8,128)(2,1)}) %all-gather.5.cloned.1.call-update) | async-done | bytes 4194320 | tf_op jit(solution)/shard_map/all_gather | solution.py:163
  208.2 5.2 %fusion.50 = f32[256,256]{0,1:T(8,128)S(1)} fusion(bf16[256,8192]{1,0:T(8,128)(2,1)} %param.21, bf16[8192,256]{1,0:T(8,128)(2,1)} %all-gather.5.cloned.1.call-done), kind=kOutput, calls=%fused_computation.122 | convolution fusion | flops 1073741824 | bytes 8650752 | tf_op jit(solution)/shard_map/dot_general | solution.py:161
  213.5 0.3 convolution_add_fusion.1
  213.9 0.1 copy.27
  214.0 2.2 scatter_custom_fusion
  216.2 3.4 %all-to-all-start = ((bf16[8,32,512]{2,1,0:T(8,128)(2,1)}), bf16[8,32,512]{2,1,0:T(8,128)(2,1)S(1)}, u32[]{:S(2)}, u32[]{:S(2)}) async-start(bf16[8,32,512]{2,1,0:T(8,128)(2,1)} %bitcast.24), calls=%async_computation | async-start | bytes 524288 | tf_op jit(solution)/shard_map/all_to_all | solution.py:183
  219.6 0.1 lt.84
  219.9 0.1 fusion.31
  220.0 0.2 fusion.48
  220.2 8.0 %all-to-all-done = bf16[8,32,512]{2,1,0:T(8,128)(2,1)S(1)} async-done(((bf16[8,32,512]{2,1,0:T(8,128)(2,1)}), bf16[8,32,512]{2,1,0:T(8,128)(2,1)S(1)}, u32[]{:S(2)}, u32[]{:S(2)}) %all-to-all-start) | async-done | bytes 262176 | tf_op jit(solution)/shard_map/all_to_all | solution.py:183
  228.3 0.2 fusion.49
  228.6 0.2 fusion.24
  228.7 0.2 fusion.7
  228.9 0.2 fusion.5
  229.2 30.5 %all-gather = bf16[8,1,2048]{2,1,0:T(2,128)(2,1)S(1)} all-gather(bf16[1,1,2048]{2,1,0:T(2,128)(2,1)S(1)} %reshape.342), channel_id=1, replica_groups=mesh['group'=2,'dev'=8,'tp'=2] {'dev'}, dimensions={0}, use_global_device_ids=true | all-gather | bytes 36864 | tf_op jit(solution)/shard_map/all_gather | solution.py:201
  259.7 2.8 %fusion.16 = f32[8,1024]{1,0:T(8,128)S(1)} fusion(bf16[2048,1024]{1,0:T(8,128)(2,1)} %param.35, bf16[8,1,2048]{2,1,0:T(2,128)(2,1)S(1)} %all-gather), kind=kOutput, calls=%fused_computation.34 | convolution fusion | flops 33554432 | bytes 4259840 | tf_op jit(solution)/shard_map/dot_general | solution.py:202
  262.5 0.2 convolution_select_fusion.1
  262.7 0.2 convolution_add_fusion.2
  262.9 4.0 %psum.7 = bf16[8,1024]{1,0:T(8,128)(2,1)} all-reduce(f32[8,1024]{1,0:T(8,128)S(1)} %convolution_add_fusion.2), channel_id=1, replica_groups=mesh['group'=2,'dev'=8,'tp'=2] {'tp'}, use_global_device_ids=true, to_apply=%region_11.14 | all-reduce | flops 8192 | bytes 49152 | tf_op jit(solution)/shard_map/psum | solution.py:207
  (47 shorter events, 0.5 us)
Async XLA Ops:
  6.5 256.0 %copy-start = (bf16[2048,64]{0,1:T(8,128)(2,1)S(1)}, bf16[2048,64]{0,1:T(8,128)(2,1)}, u32[]{:S(2)}) copy-start(bf16[2048,64]{0,1:T(8,128)(2,1)} %param.36) | copy-start | bytes 786436
  6.5 12.8 %copy-start.4 = (s32[8]{0:T(128)S(1)}, s32[8]{0:T(128)}, u32[]{:S(2)}) copy-start(s32[8]{0:T(128)} %param.29) | copy-start | bytes 100
  6.5 14.1 %copy-start.6 = (s32[8]{0:T(128)S(1)}, s32[8]{0:T(128)}, u32[]{:S(2)}) copy-start(s32[8]{0:T(128)} %param.27) | copy-start | bytes 100
  6.5 54.7 %all-gather.7.cloned.1.call-start = ((), (), s32[]{:S(2)}) async-start(), calls=%async_computation.2 | async-start | bytes 2359296 | tf_op jit(solution)/shard_map/all_gather | solution.py:165
  7.3 127.5 %all-gather.9.cloned.1.call-start = ((), (), s32[]{:S(2)}) async-start(), calls=%async_computation.3 | async-start | bytes 4718592 | tf_op jit(solution)/shard_map/all_gather | solution.py:164
  8.0 200.2 %all-gather.5.cloned.1.call-start = ((), (), s32[]{:S(2)}) async-start(), calls=%async_computation.1 | async-start | bytes 4718592 | tf_op jit(solution)/shard_map/all_gather | solution.py:163
  65.6 74.3 %copy-start.7 = (bf16[64,256]{1,0:T(8,128)(2,1)S(1)}, bf16[64,256]{1,0:T(8,128)(2,1)}, u32[]{:S(2)}) copy-start(bf16[64,256]{1,0:T(8,128)(2,1)} %param.26) | copy-start | bytes 98308
  140.3 73.2 %copy-start.5 = (bf16[64,256]{1,0:T(8,128)(2,1)S(1)}, bf16[64,256]{1,0:T(8,128)(2,1)}, u32[]{:S(2)}) copy-start(bf16[64,256]{1,0:T(8,128)(2,1)} %param.25) | copy-start | bytes 98308
  140.3 79.3 %copy-start.9 = (bf16[1,256]{1,0:T(2,128)(2,1)S(1)}, bf16[1,256]{1,0:T(2,128)(2,1)}, u32[]{:S(2)}) copy-start(bf16[1,256]{1,0:T(2,128)(2,1)} %param.32) | copy-start | bytes 1540
  140.3 79.4 %copy-start.1 = (bf16[1,256,256]{2,1,0:T(8,128)(2,1)S(1)}, bf16[1,256,256]{2,1,0:T(8,128)(2,1)}, u32[]{:S(2)}) copy-start(bf16[1,256,256]{2,1,0:T(8,128)(2,1)} %param.33) | copy-start | bytes 393220
  140.3 79.5 %copy-start.2 = (bf16[1,256,256]{2,1,0:T(8,128)(2,1)S(1)}, bf16[1,256,256]{2,1,0:T(8,128)(2,1)}, u32[]{:S(2)}) copy-start(bf16[1,256,256]{2,1,0:T(8,128)(2,1)} %param.34) | copy-start | bytes 393220
  140.3 79.5 %copy-start.8 = (bf16[1,2048]{1,0:T(2,128)(2,1)S(1)}, bf16[1,2048]{1,0:T(2,128)(2,1)}, u32[]{:S(2)}) copy-start(bf16[1,2048]{1,0:T(2,128)(2,1)} %param.30) | copy-start | bytes 12292
  140.3 79.5 %copy-start.10 = (bf16[1,256]{1,0:T(2,128)(2,1)S(1)}, bf16[1,256]{1,0:T(2,128)(2,1)}, u32[]{:S(2)}) copy-start(bf16[1,256]{1,0:T(2,128)(2,1)} %param.31) | copy-start | bytes 1540
  213.9 48.9 %copy-start.3 = (bf16[64,1024]{1,0:T(8,128)(2,1)S(1)}, bf16[64,1024]{1,0:T(8,128)(2,1)}, u32[]{:S(2)}) copy-start(bf16[64,1024]{1,0:T(8,128)(2,1)} %param.37) | copy-start | bytes 393220
  216.2 12.0 %all-to-all-start = ((bf16[8,32,512]{2,1,0:T(8,128)(2,1)}), bf16[8,32,512]{2,1,0:T(8,128)(2,1)S(1)}, u32[]{:S(2)}, u32[]{:S(2)}) async-start(bf16[8,32,512]{2,1,0:T(8,128)(2,1)} %bitcast.24), calls=%async_computation | async-start | bytes 524288 | tf_op jit(solution)/shard_map/all_to_all | solution.py:183
Sparse Core Ops, SparseCore 0:
  9.5 51.7 all-gather.6
  63.4 71.3 all-gather.8
  136.9 71.3 all-gather.4
where the time goes:
time: 274 us; the launch traced here: 273 us
  waiting for transfers between devices  177 us (65%)
  blocking collectives  34.5 us (13%)
  matrix products  19.5 us (7%)
  other arithmetic  14.3 us (5%)
  between operations  14 us (5%)
  local copies, waits for them, and re-layouts  10.7 us (4%)
  starting transfers between devices  3.49 us (1%)
    all_gather x1, waiting for transfers between devices, per_device(): lax.all_gather(value_matrix, 'dev', axis=0, tiled=True)  69.1 us
    all_gather x1, waiting for transfers between devices, per_device(): key_raw = add_rows(lax.all_gather(key_matrix, 'dev', axis=0, tiled=True))  67.9 us
    all_gather x1, blocking collectives, per_device(): portion = lax.all_gather(mixed_local, 'dev', axis=0, tiled=True)  30.5 us
    all_gather x1, waiting for transfers between devices, per_device(): lax.all_gather(adapter_down_keyvalue, 'dev', axis=0, tiled=True)  29.8 us
    dot_general x2, matrix products, add_rows(): jnp.dot(prompt_activations, portion, preferred_element_type=jnp.float32)  10.4 us
    convert_element_type x1, other arithmetic, rotate(): angles = positions.astype(jnp.float32)[:, None] * frequency[None, :]  9.74 us
    all_to_all x1, waiting for transfers between devices, per_device(): lax.all_to_all(outgoing, 'dev', split_axis=0, concat_axis=0, tiled=True)  8 us
  transfers between devices with their start and end apart: 4, of which 4 were waited for; matrix products, arithmetic and copies ran while one was open for 12% of the time, Pallas kernels for 0%

commit v1 on v0

--- a/solution.py
+++ b/solution.py
@@ -1,6 +1,10 @@
+import functools
+
 import jax
 import jax.numpy as jnp
 from jax import lax
+from jax.experimental import pallas as pl
+from jax.experimental.pallas import tpu as pltpu
 from jax.sharding import PartitionSpec as P
 
 HEADS = 32
@@ -207,9 +211,469 @@
     return lax.psum(partial_output, "tp").astype(jnp.bfloat16)
 
 
+def iota(shape, axis):
+    return lax.broadcasted_iota(jnp.int32, shape, axis)
+
+
+def dot32(a, b):
+    return jnp.dot(a, b, preferred_element_type=jnp.float32)
+
+
+def dot_rows(a, b):
+    return lax.dot_general(a, b, (((1,), (1,)), ((), ())), preferred_element_type=jnp.float32)
+
+
+def halves(value):
+    high = value.astype(jnp.bfloat16)
+    return high, (value - high.astype(jnp.float32)).astype(jnp.bfloat16)
+
+
+def fused_kernel(
+    devices,
+    side,
+    capacity,
+    x_hbm,
+    wk_hbm,
+    wv_hbm,
+    ad_hbm,
+    upk_ref,
+    upv_ref,
+    adapter_ref,
+    owner_ref,
+    context_ref,
+    query_ref,
+    lastk_ref,
+    lastv_ref,
+    oldk_hbm,
+    oldv_hbm,
+    wo_hbm,
+    ado_hbm,
+    auo_hbm,
+    out_ref,
+    xr,
+    wcat,
+    upcat,
+    token_owner,
+    sent,
+    got,
+    oldk,
+    oldv,
+    wo,
+    ado,
+    auo,
+    mixes,
+    part,
+    other,
+    local_sem,
+    xs_sem,
+    xr_sem,
+    fs_sem,
+    fr_sem,
+    ps_sem,
+    pr_sem,
+    ms_sem,
+    mr_sem,
+    ts_sem,
+    tr_sem,
+):
+    group = lax.axis_index("group")
+    me = lax.axis_index("dev")
+    core = lax.axis_index("tp")
+    partner = (group, me, 1 - core)
+    rows = owner_ref.shape[0]
+    tok = x_hbm.shape[0]
+    depth = wk_hbm.shape[0]
+    width = wk_hbm.shape[1]
+    low = ad_hbm.shape[1]
+    half = tok // 2
+    slots = capacity * PAGE
+    outer = devices // side
+    mz, mx = me // side, me % side
+
+    def ahead(k):
+        return ((mz + k // side) % outer) * side + (mx + k % side) % side
+
+    def behind(k):
+        return ((mz + outer - k // side) % outer) * side + (mx + side - k % side) % side
+
+    own_half = pl.ds(pl.multiple_of(core * half, half), half)
+
+    locals_ = [
+        pltpu.make_async_copy(
+            x_hbm.at[:, pl.ds(pl.multiple_of(me * depth, depth), depth)], xr.at[0], local_sem.at[0]
+        ),
+        pltpu.make_async_copy(wk_hbm, wcat.at[:, pl.ds(0, width)], local_sem.at[1]),
+        pltpu.make_async_copy(wv_hbm, wcat.at[:, pl.ds(width, width)], local_sem.at[2]),
+        pltpu.make_async_copy(ad_hbm, wcat.at[:, pl.ds(2 * width, low)], local_sem.at[3]),
+        pltpu.make_async_copy(oldk_hbm, oldk, local_sem.at[4]),
+        pltpu.make_async_copy(oldv_hbm, oldv, local_sem.at[5]),
+        pltpu.make_async_copy(wo_hbm, wo, local_sem.at[6]),
+        pltpu.make_async_copy(ado_hbm, ado, local_sem.at[7]),
+        pltpu.make_async_copy(auo_hbm, auo, local_sem.at[8]),
+    ]
+    for copy in locals_[:4]:
+        copy.start()
+
+    barrier = pltpu.get_barrier_semaphore()
+    for k in range(1, devices):
+        pl.semaphore_signal(
+            barrier, inc=1, device_id=(group, ahead(k), core), device_id_type=pl.DeviceIdType.MESH
+        )
+    pl.semaphore_signal(barrier, inc=1, device_id=partner, device_id_type=pl.DeviceIdType.MESH)
+    pl.semaphore_wait(barrier, devices)
+
+    def x_copy(k):
+        peer = ahead(k)
+        return pltpu.make_async_remote_copy(
+            src_ref=x_hbm.at[own_half, pl.ds(pl.multiple_of(peer * depth, depth), depth)],
+            dst_ref=xr.at[k, own_half],
+            send_sem=xs_sem.at[k],
+            recv_sem=xr_sem.at[k],
+            device_id=(group, peer, core),
+            device_id_type=pl.DeviceIdType.MESH,
+        )
+
+    def forward(k):
+        return pltpu.make_async_remote_copy(
+            src_ref=xr.at[k, own_half],
+            dst_ref=xr.at[k, own_half],
+            send_sem=fs_sem.at[k],
+            recv_sem=fr_sem.at[k],
+            device_id=partner,
+            device_id_type=pl.DeviceIdType.MESH,
+        )
+
+    def part_copy(k, o):
+        peer = ahead(o)
+        source = behind(k)
+        return pltpu.make_async_remote_copy(
+            src_ref=sent.at[k, pl.ds(pl.multiple_of(peer * slots, slots), slots)],
+            dst_ref=got.at[o, pl.ds(pl.multiple_of(source * slots, slots), slots)],
+            send_sem=ps_sem.at[k, o],
+            recv_sem=pr_sem.at[k, o],
+            device_id=(group, peer, core),
+            device_id_type=pl.DeviceIdType.MESH,
+        )
+
+    for k in range(1, devices):
+        x_copy(k).start()
+    for copy in locals_[4:]:
+        copy.start()
+
+    pages = owner_ref.shape[1]
+    spread = (iota((pages, tok), 1) // PAGE == iota((pages, tok), 0)).astype(jnp.bfloat16)
+    token_owner[...] = dot32(owner_ref[...].astype(jnp.float32).astype(jnp.bfloat16), spread)
+    earlier = (iota((tok, tok), 0) // PAGE < iota((tok, tok), 1) // PAGE).astype(jnp.bfloat16)
+    lora = low // 2
+    upcat[...] = jnp.zeros_like(upcat)
+    upcat[pl.ds(0, lora), pl.ds(0, width)] = upk_ref[...]
+    upcat[pl.ds(lora, lora), pl.ds(width, width)] = upv_ref[...]
+    adapters = adapter_ref[...].astype(jnp.float32)
+    slot_rows = devices * slots
+    row_adapter = jnp.sum(
+        jnp.where(iota((slot_rows, devices), 0) // slots == iota((slot_rows, devices), 1), adapters, 0.0),
+        axis=1,
+        keepdims=True,
+    )
+    low_adapter = ((iota((slot_rows, low), 1) % lora) // LOW_RANK).astype(jnp.float32)
+    keep_low = low_adapter == row_adapter
+
+    for copy in locals_[:4]:
+        copy.wait()
+
+    def step(k, carry):
+        @pl.when(k < devices - 1)
+        def _():
+            x_copy(k + 1).wait_recv()
+            forward(k + 1).start()
+
+        @pl.when(k > 0)
+        def _():
+            forward(k).wait_recv()
+
+        source = behind(k)
+        owners = token_owner[pl.ds(source, 1), :]
+        hot = iota((devices, tok), 0).astype(jnp.float32) == owners
+        hot32 = hot.astype(jnp.float32)
+        before = dot32(hot32.astype(jnp.bfloat16), earlier)
+        rank = jnp.sum(before * hot32, axis=0, keepdims=True)
+        place = (
+            owners * float(slots) + rank + (iota((1, tok), 1) % PAGE).astype(jnp.float32)
+        )
+        move = (iota((slot_rows, tok), 0).astype(jnp.float32) == place).astype(jnp.bfloat16)
+        ordered = dot32(move, xr[k]).astype(jnp.bfloat16)
+        wide = dot32(ordered, wcat[...])
+        high, rest = halves(jnp.where(keep_low, wide[:, 2 * width :], 0.0))
+        total = wide[:, : 2 * width] + dot32(high, upcat[...]) + dot32(rest, upcat[...])
+        sent[k] = total.astype(jnp.bfloat16)
+        for o in range(1, devices):
+            part_copy(k, o).start()
+        got[0, pl.ds(pl.multiple_of(source * slots, slots), slots), :] = sent[
+            k, pl.ds(pl.multiple_of(me * slots, slots), slots), :
+        ]
+        return carry
+
+    lax.fori_loop(0, devices, step, 0)
+
+    mine = (token_owner[...] == me.astype(jnp.float32)).astype(jnp.float32)
+    fresh = devices * slots
+    prior = (iota((fresh, devices), 1) < iota((fresh, devices), 0) // slots).astype(jnp.float32)
+    past = jnp.sum(
+        dot32(prior.astype(jnp.bfloat16), mine.astype(jnp.bfloat16)), axis=1, keepdims=True
+    )
+    context = jnp.sum(
+        jnp.where(iota((1, devices), 1) == me, context_ref[...].astype(jnp.float32), 0.0),
+        axis=1,
+        keepdims=True,
+    )
+    position = context + past + (iota((fresh, 1), 0) % slots).astype(jnp.float32)
+    count = jnp.sum(mine, axis=1, keepdims=True)
+    fresh_count = jnp.sum(
+        jnp.where(iota((devices, fresh), 1) // slots == iota((devices, fresh), 0), count, 0.0),
+        axis=0,
+        keepdims=True,
+    )
+    fresh_valid = (iota((1, fresh), 1) % slots).astype(jnp.float32) < fresh_count
+    half_size = HEAD // 2
+    lane = iota((1, HEAD), 1)
+    exponent = (lane % half_size).astype(jnp.float32) * (2.0 / HEAD)
+    frequency = jnp.exp(-jnp.log(jnp.full((1, HEAD), rope_base, jnp.float32)) * exponent)
+    angle = position * frequency
+    cosine = jnp.cos(angle)
+    sine = jnp.sin(angle)
+    sine = jnp.where(lane < half_size, -sine, sine)
+
+    for copy in locals_[4:]:
+        copy.wait()
+    kv_local = width // HEAD
+    members = HEADS // KV_HEADS
+    scale = HEAD ** (-0.5)
+    query = query_ref[...].astype(jnp.float32)
+    old_count = oldk.shape[0]
+    old_valid = iota((1, old_count), 1).astype(jnp.float32) < context
+    queries, old_scores, last_scores = [], [], []
+    for h in range(kv_local):
+        heads = jnp.concatenate(
+            [query[:, (h * members + g) * HEAD : (h * members + g + 1) * HEAD] for g in range(members)],
+            axis=0,
+        )
+        cols = slice(h * HEAD, (h + 1) * HEAD)
+        queries.append(heads.astype(jnp.bfloat16))
+        old_scores.append(
+            jnp.where(old_valid, dot_rows(queries[h], oldk[:, cols]) * scale, -1e30)
+        )
+        last_scores.append(
+            jnp.sum(heads * lastk_ref[:, cols].astype(jnp.float32), axis=1, keepdims=True) * scale
+        )
+
+    def settle(k, carry):
+        for o in range(1, devices):
+            part_copy(k, o).wait_recv()
+        return carry
+
+    lax.fori_loop(0, devices, settle, 0)
+    for h in range(kv_local):
+        cols = slice(h * HEAD, (h + 1) * HEAD)
+        key = got[0, :, cols].astype(jnp.float32)
+        value = got[0, :, width + h * HEAD : width + (h + 1) * HEAD].astype(jnp.float32)
+        for o in range(1, devices):
+            key = key + got[o, :, cols].astype(jnp.float32)
+            value = value + got[o, :, width + h * HEAD : width + (h + 1) * HEAD].astype(jnp.float32)
+        key = (key * cosine + pltpu.roll(key, half_size, 1) * sine).astype(jnp.bfloat16)
+        value = value.astype(jnp.bfloat16)
+        fresh_scores = jnp.where(fresh_valid, dot_rows(queries[h], key) * scale, -1e30)
+        top = jnp.maximum(
+            jnp.maximum(
+                jnp.max(old_scores[h], axis=1, keepdims=True),
+                jnp.max(fresh_scores, axis=1, keepdims=True),
+            ),
+            last_scores[h],
+        )
+        old_weights = jnp.exp(old_scores[h] - top)
+        fresh_weights = jnp.exp(fresh_scores - top)
+        last_weight = jnp.exp(last_scores[h] - top)
+        total = (
+            jnp.sum(old_weights, axis=1, keepdims=True)
+            + jnp.sum(fresh_weights, axis=1, keepdims=True)
+            + last_weight
+        )
+        mixed = dot32((old_weights / total).astype(jnp.bfloat16), oldv[:, cols])
+        mixed = mixed + dot32((fresh_weights / total).astype(jnp.bfloat16), value)
+        mixed = mixed + (last_weight / total).astype(jnp.bfloat16).astype(jnp.float32) * lastv_ref[
+            :, cols
+        ].astype(jnp.float32)
+        mixes[me, pl.ds(h * members, members), :] = mixed.astype(jnp.bfloat16).astype(jnp.float32)
+
+    def mix_copy(o, row):
+        return pltpu.make_async_remote_copy(
+            src_ref=mixes.at[row],
+            dst_ref=mixes.at[row],
+            send_sem=ms_sem.at[o],
+            recv_sem=mr_sem.at[o],
+            device_id=(group, ahead(o), core),
+            device_id_type=pl.DeviceIdType.MESH,
+        )
+
+    for o in range(1, devices):
+        mix_copy(o, me).start()
+    for o in range(1, devices):
+        mix_copy(o, behind(o)).wait_recv()
+    everyone = jnp.concatenate(
+        [mixes[:, h, :] for h in range(kv_local * members)], axis=1
+    ).astype(jnp.bfloat16)
+    narrowed = dot32(everyone, ado[...])
+    row_of = jnp.sum(
+        jnp.where(iota((devices, devices), 0) == iota((devices, devices), 1), adapters, 0.0),
+        axis=1,
+        keepdims=True,
+    )
+    narrow_adapter = (
+        (iota((devices, narrowed.shape[1]), 1) % (ADAPTER_COUNT * LOW_RANK)) // LOW_RANK
+    ).astype(jnp.float32)
+    high, rest = halves(jnp.where(narrow_adapter == row_of, narrowed, 0.0))
+    part[...] = dot32(everyone, wo[...]) + dot32(high, auo[...]) + dot32(rest, auo[...])
+    swap = pltpu.make_async_remote_copy(
+        src_ref=part,
+        dst_ref=other,
+        send_sem=ts_sem,
+        recv_sem=tr_sem,
+        device_id=partner,
+        device_id_type=pl.DeviceIdType.MESH,
+    )
+    swap.start()
+
+    for k in range(1, devices):
+        x_copy(k).wait_send()
+        forward(k).wait_send()
+        mix_copy(k, me).wait_send()
+
+    def drain(k, carry):
+        for o in range(1, devices):
+            part_copy(k, o).wait_send()
+        return carry
+
+    lax.fori_loop(0, devices, drain, 0)
+    swap.wait()
+    out_ref[...] = (part[...] + other[...]).astype(jnp.bfloat16)
+
+
+def fused(
+    side,
+    prompt_activations,
+    key_matrix,
+    value_matrix,
+    adapter_down_keyvalue,
+    adapter_up_key,
+    adapter_up_value,
+    request_adapter,
+    page_request,
+    context_tokens,
+    step_query,
+    step_key,
+    step_value,
+    stored_keys,
+    stored_values,
+    output_matrix,
+    adapter_down_output,
+    adapter_up_output,
+):
+    devices = lax.axis_size("dev")
+    tok, _ = prompt_activations.shape
+    depth, width = key_matrix.shape
+    low = adapter_down_keyvalue.shape[1]
+    capacity = slots_of(tok // PAGE, devices)
+    slots = capacity * PAGE
+    rows = request_adapter.shape[0]
+    heads = step_query.shape[1] // HEAD
+    out_width = output_matrix.shape[1]
+    bf16, f32 = jnp.bfloat16, jnp.float32
+    whole = pl.BlockSpec(memory_space=pltpu.VMEM)
+    far = pl.BlockSpec(memory_space=pl.ANY)
+    dma = pltpu.SemaphoreType.DMA
+    return pl.pallas_call(
+        functools.partial(fused_kernel, devices, side, capacity),
+        out_shape=jax.ShapeDtypeStruct((rows, out_width), bf16),
+        in_specs=[far] * 4 + [whole] * 8 + [far] * 5,
+        out_specs=whole,
+        scratch_shapes=[
+            pltpu.VMEM((devices, tok, depth), bf16),
+            pltpu.VMEM((depth, 2 * width + low), bf16),
+            pltpu.VMEM((low, 2 * width), bf16),
+            pltpu.VMEM((devices, tok), f32),
+            pltpu.VMEM((devices, devices * slots, 2 * width), bf16),
+            pltpu.VMEM((devices, devices * slots, 2 * width), bf16),
+            pltpu.VMEM(stored_keys.shape[1:], bf16),
+            pltpu.VMEM(stored_values.shape[1:], bf16),
+            pltpu.VMEM(output_matrix.shape, bf16),
+            pltpu.VMEM(adapter_down_output.shape, bf16),
+            pltpu.VMEM(adapter_up_output.shape, bf16),
+            pltpu.VMEM((devices, heads, HEAD), f32),
+            pltpu.VMEM((rows, out_width), f32),
+            pltpu.VMEM((rows, out_width), f32),
+            dma((9,)),
+            dma((devices,)),
+            dma((devices,)),
+            dma((devices,)),
+            dma((devices,)),
+            dma((devices, devices)),
+            dma((devices, devices)),
+            dma((devices,)),
+            dma((devices,)),
+            dma,
+            dma,
+        ],
+        compiler_params=pltpu.CompilerParams(
+            collective_id=0, has_side_effects=True, vmem_limit_bytes=60 * 1024 * 1024
+        ),
+    )(
+        prompt_activations,
+        key_matrix,
+        value_matrix,
+        adapter_down_keyvalue,
+        adapter_up_key,
+        adapter_up_value,
+        request_adapter.reshape(1, -1),
+        page_request.reshape(devices, -1),
+        context_tokens.reshape(1, -1),
+        step_query,
+        step_key,
+        step_value,
+        stored_keys[0],
+        stored_values[0],
+        output_matrix,
+        adapter_down_output,
+        adapter_up_output,
+    )
+
+
+def slots_of(pages_here, devices):
+    return max(2, (pages_here + devices - 1) // devices)
+
+
+def choose(*args):
+    devices = lax.axis_size("dev")
+    tok = args[0].shape[0]
+    depth, width = args[1].shape
+    slots = slots_of(tok // PAGE, devices) * PAGE
+    fits = (
+        lax.axis_size("tp") == 2
+        and args[6].shape[0] == devices
+        and devices % 2 == 0
+        and devices <= 16
+        and devices * slots == tok
+        and tok <= 256
+        and depth % 128 == 0
+        and width % HEAD == 0
+        and slots % 16 == 0
+    )
+    if fits:
+        return fused(2, *args)
+    return per_device(*args)
+
+
 def solution(mesh):
     return jax.shard_map(
-        per_device,
+        choose,
         mesh=mesh,
         in_specs=(
             P(("group", "dev"), None),

time: 274 us -> 114 us (0.42)
  waiting for transfers between devices: 177 us -> 0 us
  Pallas kernels: 0 us -> 108 us
  blocking collectives: 34.5 us -> 0 us
  matrix products: 19.5 us -> 0 us
  between operations: 14 us -> 0.01 us
  other arithmetic: 14.3 us -> 1.34 us
  local copies, waits for them, and re-layouts: 10.7 us -> 4.45 us
  starting transfers between devices: 3.49 us -> 0 us
    all_gather x3 -> x0, waiting for transfers between devices: 167 us -> none  [the longest x1 69.1 us: per_device(): lax.all_gather(value_matrix, 'dev', axis=0, tiled=True)]
    pallas_call x0 -> x1, Pallas kernels: none -> 108 us  [fused(): pl.pallas_call(functools.partial(fused_kernel, devices, side, capacity),...]
    all_gather x1 -> x0, blocking collectives: 30.5 us -> none  [per_device(): portion = lax.all_gather(mixed_local, 'dev', axis=0, tiled=True)]
    dot_general x13 -> x0, matrix products: 19.5 us -> none  [the longest x2 10.4 us: add_rows(): jnp.dot(prompt_activations, portion, preferred_element_type=jnp.float32)]
    convert_element_type x4 -> x0, other arithmetic: 11.2 us -> none  [the longest x1 9.74 us: rotate(): angles = positions.astype(jnp.float32)[:, None] * frequency[None, :]]
    all_to_all x1 -> x0, waiting for transfers between devices: 8 us -> none  [per_device(): lax.all_to_all(outgoing, 'dev', split_axis=0, concat_axis=0, tiled=True)]
    gather x5 -> x0, local copies, waits for them, and re-layouts: 6.95 us -> none  [the longest x1 1.88 us: per_device(): jnp.take(local_slot, token_page) * PAGE]
    psum x1 -> x0, blocking collectives: 3.99 us -> none  [per_device(): return lax.psum(partial_output, 'tp').astype(jnp.bfloat16)]
  transfers between devices with their start and end apart: 4 -> 0, of which waited for: 4 -> 0; matrix products, arithmetic and copies ran while one was open for 12% -> 0% of each run, Pallas kernels for 0% -> 0%
where the time goes in v1:
time: 114 us
  Pallas kernels  108 us (95%)
  local copies, waits for them, and re-layouts  4.45 us (4%)
  other arithmetic  1.34 us (1%)
    pallas_call x1, Pallas kernels, fused(): pl.pallas_call(functools.partial(fused_kernel, devices, side, capacity),...  108 us
    unnamed x3, local copies, waits for them, and re-layouts  3.78 us

profile of v1, /device:TPU:0, one launch (start us, length us, event | category | flops | bytes accessed | tf_op | source)
XLA Modules:
  0.0 113.7 jit_solution(13428791575714998502)
XLA Ops:
  0.0 0.5 broadcast.3
  0.5 1.3 %reduce.3 = s32[512]{0:T(512)S(1)} reduce(s32[512,1]{0,1:T(1,128)} %param.24, s32[]{:T(128)} %broadcast.3), dimensions={1}, to_apply=%param.24.reduce_sub_computation.3 | reduce | bytes 4100 | tf_op args[7]
  1.9 0.7 reshape.10.owner_ref
  2.5 1.9 %copy.18.ado_hbm = bf16[2048,64]{1,0:T(8,128)(2,1)} copy(bf16[2048,64]{0,1:T(8,128)(2,1)} %param.32) | data formatting | bytes 524288 | tf_op args[15]
  4.5 107.9 %shard_map.163 = bf16[8,1024]{1,0:T(8,128)(2,1)} custom-call(bf16[256,8192]{1,0:T(8,128)(2,1)} %x_hbm.1, bf16[1024,256]{1,0:T(8,128)(2,1)} %wk_hbm.1, bf16[1024,256]{1,0:T(8,128)(2,1)} %wv_hbm.1, bf16[1024,128]{1,0:T(8,128)(2,1)} %ad_hbm.1, bf16[64,256]{1,0:T(8,128)(2,1)} %upk_ref.1, bf16[64,256]{1,0:T(8,128)(2,1)} %upv_ref.1, s32[1,8]{1,0:T(1,128)} %bitcast.7, ...), custom_call_target="tpu_custom_call" | custom-call | tf_op jit(solution)/shard_map/pallas_call | solution.py:593
  112.4 1.3 %copy.20 = bf16[8,1024]{1,0:T(8,128)(2,1)} copy(bf16[8,1024]{1,0:T(8,128)(2,1)} %shard_map.163) | data formatting | bytes 32768

commit v2 on v1

--- a/solution.py
+++ b/solution.py
@@ -250,10 +250,13 @@
     ado_hbm,
     auo_hbm,
     out_ref,
-    xr,
-    wcat,
+    raw,
+    acts,
+    weights,
     upcat,
     token_owner,
+    shipped,
+    landed,
     sent,
     got,
     oldk,
@@ -269,6 +272,14 @@
     xr_sem,
     fs_sem,
     fr_sem,
+    zs_sem,
+    zr_sem,
+    ys_sem,
+    yr_sem,
+    qs_sem,
+    qr_sem,
+    es_sem,
+    er_sem,
     ps_sem,
     pr_sem,
     ms_sem,
@@ -280,7 +291,6 @@
     me = lax.axis_index("dev")
     core = lax.axis_index("tp")
     partner = (group, me, 1 - core)
-    rows = owner_ref.shape[0]
     tok = x_hbm.shape[0]
     depth = wk_hbm.shape[0]
     width = wk_hbm.shape[1]
@@ -289,6 +299,11 @@
     slots = capacity * PAGE
     outer = devices // side
     mz, mx = me // side, me % side
+    beside = (group, mz * side + 1 - mx, core)
+    across = (1 - group, me, core)
+    kv_local = width // HEAD
+    chunks = 1 + 2 * kv_local
+    mesh_ids = pl.DeviceIdType.MESH
 
     def ahead(k):
         return ((mz + k // side) % outer) * side + (mx + k % side) % side
@@ -296,68 +311,182 @@
     def behind(k):
         return ((mz + outer - k // side) % outer) * side + (mx + side - k % side) % side
 
+    def source_of(j):
+        if j == 0:
+            return ad_hbm, 0
+        if j <= kv_local:
+            return wk_hbm, (j - 1) * HEAD
+        return wv_hbm, (j - 1 - kv_local) * HEAD
+
+    def rows_of(j, cut):
+        if j == 0:
+            size = depth // 4
+            return pl.ds(pl.multiple_of((cut * 2 + core) * size, size), size)
+        size = depth // 2
+        return pl.ds(pl.multiple_of(cut * size, size), size)
+
+    def remote(src, dst, send, recv, device):
+        return pltpu.make_async_remote_copy(
+            src_ref=src,
+            dst_ref=dst,
+            send_sem=send,
+            recv_sem=recv,
+            device_id=device,
+            device_id_type=mesh_ids,
+        )
+
     own_half = pl.ds(pl.multiple_of(core * half, half), half)
 
-    locals_ = [
-        pltpu.make_async_copy(
-            x_hbm.at[:, pl.ds(pl.multiple_of(me * depth, depth), depth)], xr.at[0], local_sem.at[0]
-        ),
-        pltpu.make_async_copy(wk_hbm, wcat.at[:, pl.ds(0, width)], local_sem.at[1]),
-        pltpu.make_async_copy(wv_hbm, wcat.at[:, pl.ds(width, width)], local_sem.at[2]),
-        pltpu.make_async_copy(ad_hbm, wcat.at[:, pl.ds(2 * width, low)], local_sem.at[3]),
-        pltpu.make_async_copy(oldk_hbm, oldk, local_sem.at[4]),
-        pltpu.make_async_copy(oldv_hbm, oldv, local_sem.at[5]),
-        pltpu.make_async_copy(wo_hbm, wo, local_sem.at[6]),
-        pltpu.make_async_copy(ado_hbm, ado, local_sem.at[7]),
-        pltpu.make_async_copy(auo_hbm, auo, local_sem.at[8]),
-    ]
-    for copy in locals_[:4]:
-        copy.start()
+    def columns(b, x):
+        return pl.ds(pl.multiple_of((b * side + x) * depth, depth), depth)
+
+    locals_ = []
+    for j in range(chunks):
+        ref, at = source_of(j)
+        locals_.append(
+            pltpu.make_async_copy(ref.at[:, pl.ds(at, HEAD)], weights.at[j, mz], local_sem.at[j])
+        )
+    for b in range(outer):
+        locals_.append(
+            pltpu.make_async_copy(
+                x_hbm.at[:, columns(b, mx)], raw.at[0, b], local_sem.at[chunks + b]
+            )
+        )
+    rest_at = chunks + outer
+    later = [(oldk_hbm, oldk), (oldv_hbm, oldv), (wo_hbm, wo), (ado_hbm, ado), (auo_hbm, auo)]
+    for i, (ref, to) in enumerate(later):
+        locals_.append(pltpu.make_async_copy(ref, to, local_sem.at[rest_at + i]))
 
     barrier = pltpu.get_barrier_semaphore()
     for k in range(1, devices):
         pl.semaphore_signal(
-            barrier, inc=1, device_id=(group, ahead(k), core), device_id_type=pl.DeviceIdType.MESH
-        )
-    pl.semaphore_signal(barrier, inc=1, device_id=partner, device_id_type=pl.DeviceIdType.MESH)
-    pl.semaphore_wait(barrier, devices)
-
-    def x_copy(k):
-        peer = ahead(k)
-        return pltpu.make_async_remote_copy(
-            src_ref=x_hbm.at[own_half, pl.ds(pl.multiple_of(peer * depth, depth), depth)],
-            dst_ref=xr.at[k, own_half],
-            send_sem=xs_sem.at[k],
-            recv_sem=xr_sem.at[k],
-            device_id=(group, peer, core),
-            device_id_type=pl.DeviceIdType.MESH,
-        )
-
-    def forward(k):
-        return pltpu.make_async_remote_copy(
-            src_ref=xr.at[k, own_half],
-            dst_ref=xr.at[k, own_half],
-            send_sem=fs_sem.at[k],
-            recv_sem=fr_sem.at[k],
-            device_id=partner,
-            device_id_type=pl.DeviceIdType.MESH,
-        )
-
-    def part_copy(k, o):
+            barrier, inc=1, device_id=(group, ahead(k), core), device_id_type=mesh_ids
+        )
+    pl.semaphore_signal(barrier, inc=1, device_id=partner, device_id_type=mesh_ids)
+    pl.semaphore_signal(barrier, inc=1, device_id=across, device_id_type=mesh_ids)
+    pl.semaphore_wait(barrier, devices + 1)
+
+    def x_copy(b):
+        return remote(
+            x_hbm.at[own_half, columns(b, 1 - mx)],
+            raw.at[1, b, own_half],
+            xs_sem.at[b],
+            xr_sem.at[b],
+            beside,
+        )
+
+    def x_forward(b):
+        view = raw.at[1, b, own_half]
+        return remote(view, view, fs_sem.at[b], fr_sem.at[b], partner)
+
+    def z_first(j, up):
+        ref, at = source_of(j)
+        to = mz + 1 if up else mz - 1
+        return remote(
+            ref.at[rows_of(j, group), pl.ds(at, HEAD)],
+            weights.at[j, mz, rows_of(j, group)],
+            zs_sem.at[j, mz, 0 if up else 1],
+            zr_sem.at[j, mz],
+            (group, to * side + mx, core),
+        )
+
+    def z_relay(j, b, up):
+        view = weights.at[j, b, rows_of(j, group)]
+        to = mz + 1 if up else mz - 1
+        return remote(
+            view,
+            view,
+            zs_sem.at[j, b, 0 if up else 1],
+            zr_sem.at[j, b],
+            (group, to * side + mx, core),
+        )
+
+    def y_copy(j, b):
+        view = weights.at[j, b, rows_of(j, group)]
+        return remote(view, view, ys_sem.at[j, b], yr_sem.at[j, b], across)
+
+    def y_arrival(j, b):
+        view = weights.at[j, b, rows_of(j, 1 - group)]
+        return remote(view, view, ys_sem.at[j, b], yr_sem.at[j, b], across)
+
+    def q_copy(b, cut, which):
+        view = weights.at[0, b, rows_of(0, cut)]
+        return remote(view, view, qs_sem.at[b, which], qr_sem.at[b, which], partner)
+
+    def issue(j):
+        @pl.when(mz < outer - 1)
+        def _():
+            z_first(j, True).start()
+
+        @pl.when(mz > 0)
+        def _():
+            z_first(j, False).start()
+
+    def relay(j):
+        for t in range(1, outer):
+            for up in (True, False):
+                b = mz - t if up else mz + t
+
+                @pl.when(b >= 0 if up else b < outer)
+                def _():
+                    z_relay(j, b, up).wait_recv()
+
+                    @pl.when(mz < outer - 1 if up else mz > 0)
+                    def _():
+                        z_relay(j, b, up).start()
+
+                    y_copy(j, b).start()
+                    if j == 0:
+                        q_copy(b, group, 0).start()
+
+    def others(body):
+        for t in range(1, outer):
+            body((mz + t) % outer)
+
+    def gather(j):
+        if j == 0:
+
+            def pass_on(b):
+                y_arrival(0, b).wait_recv()
+                q_copy(b, 1 - group, 1).start()
+
+            def take(b):
+                q_copy(b, group, 0).wait_recv()
+                q_copy(b, 1 - group, 1).wait_recv()
+
+            others(pass_on)
+            others(take)
+        else:
+            others(lambda b: y_arrival(j, b).wait_recv())
+
+    def part_copy(j, o):
         peer = ahead(o)
-        source = behind(k)
-        return pltpu.make_async_remote_copy(
-            src_ref=sent.at[k, pl.ds(pl.multiple_of(peer * slots, slots), slots)],
-            dst_ref=got.at[o, pl.ds(pl.multiple_of(source * slots, slots), slots)],
-            send_sem=ps_sem.at[k, o],
-            recv_sem=pr_sem.at[k, o],
-            device_id=(group, peer, core),
-            device_id_type=pl.DeviceIdType.MESH,
-        )
-
-    for k in range(1, devices):
-        x_copy(k).start()
-    for copy in locals_[4:]:
+        return remote(
+            sent.at[j, pl.ds(pl.multiple_of(peer * slots, slots), slots)],
+            got.at[j, pl.ds(pl.multiple_of(me * slots, slots), slots)],
+            ps_sem.at[j, o],
+            pr_sem.at[j, o],
+            (group, peer, core),
+        )
+
+    def part_arrival(j, o):
+        peer = behind(o)
+        return remote(
+            sent.at[j, pl.ds(pl.multiple_of(peer * slots, slots), slots)],
+            got.at[j, pl.ds(pl.multiple_of(peer * slots, slots), slots)],
+            ps_sem.at[j, o],
+            pr_sem.at[j, o],
+            (group, peer, core),
+        )
+
+    def exchange(j):
+        return remote(shipped.at[j], landed.at[j], es_sem.at[j], er_sem.at[j], beside)
+
+    issue(0)
+    issue(1)
+    for b in range(outer):
+        x_copy(b).start()
+    for copy in locals_:
         copy.start()
 
     pages = owner_ref.shape[1]
@@ -365,6 +494,7 @@
     token_owner[...] = dot32(owner_ref[...].astype(jnp.float32).astype(jnp.bfloat16), spread)
     earlier = (iota((tok, tok), 0) // PAGE < iota((tok, tok), 1) // PAGE).astype(jnp.bfloat16)
     lora = low // 2
+    fresh = devices * slots
     upcat[...] = jnp.zeros_like(upcat)
     upcat[pl.ds(0, lora), pl.ds(0, width)] = upk_ref[...]
     upcat[pl.ds(lora, lora), pl.ds(width, width)] = upv_ref[...]
@@ -378,62 +508,30 @@
     low_adapter = ((iota((slot_rows, low), 1) % lora) // LOW_RANK).astype(jnp.float32)
     keep_low = low_adapter == row_adapter
 
-    for copy in locals_[:4]:
-        copy.wait()
-
-    def step(k, carry):
-        @pl.when(k < devices - 1)
-        def _():
-            x_copy(k + 1).wait_recv()
-            forward(k + 1).start()
-
-        @pl.when(k > 0)
-        def _():
-            forward(k).wait_recv()
-
-        source = behind(k)
+    def mover(source):
         owners = token_owner[pl.ds(source, 1), :]
-        hot = iota((devices, tok), 0).astype(jnp.float32) == owners
-        hot32 = hot.astype(jnp.float32)
-        before = dot32(hot32.astype(jnp.bfloat16), earlier)
-        rank = jnp.sum(before * hot32, axis=0, keepdims=True)
-        place = (
-            owners * float(slots) + rank + (iota((1, tok), 1) % PAGE).astype(jnp.float32)
-        )
-        move = (iota((slot_rows, tok), 0).astype(jnp.float32) == place).astype(jnp.bfloat16)
-        ordered = dot32(move, xr[k]).astype(jnp.bfloat16)
-        wide = dot32(ordered, wcat[...])
-        high, rest = halves(jnp.where(keep_low, wide[:, 2 * width :], 0.0))
-        total = wide[:, : 2 * width] + dot32(high, upcat[...]) + dot32(rest, upcat[...])
-        sent[k] = total.astype(jnp.bfloat16)
-        for o in range(1, devices):
-            part_copy(k, o).start()
-        got[0, pl.ds(pl.multiple_of(source * slots, slots), slots), :] = sent[
-            k, pl.ds(pl.multiple_of(me * slots, slots), slots), :
-        ]
-        return carry
-
-    lax.fori_loop(0, devices, step, 0)
-
-    mine = (token_owner[...] == me.astype(jnp.float32)).astype(jnp.float32)
-    fresh = devices * slots
-    prior = (iota((fresh, devices), 1) < iota((fresh, devices), 0) // slots).astype(jnp.float32)
-    past = jnp.sum(
-        dot32(prior.astype(jnp.bfloat16), mine.astype(jnp.bfloat16)), axis=1, keepdims=True
-    )
-    context = jnp.sum(
-        jnp.where(iota((1, devices), 1) == me, context_ref[...].astype(jnp.float32), 0.0),
+        hot = (iota((devices, tok), 0).astype(jnp.float32) == owners).astype(jnp.float32)
+        before = dot32(hot.astype(jnp.bfloat16), earlier)
+        rank = jnp.sum(before * hot, axis=0, keepdims=True)
+        place = owners * float(slots) + rank + (iota((1, tok), 1) % PAGE).astype(jnp.float32)
+        return (iota((fresh, tok), 0).astype(jnp.float32) == place).astype(jnp.bfloat16)
+
+    row_owner = (iota((fresh, 1), 0) // slots).astype(jnp.float32)
+    contexts = context_ref[...].astype(jnp.float32)
+    start_at = jnp.sum(
+        jnp.where(iota((fresh, devices), 0) // slots == iota((fresh, devices), 1), contexts, 0.0),
         axis=1,
         keepdims=True,
     )
-    position = context + past + (iota((fresh, 1), 0) % slots).astype(jnp.float32)
-    count = jnp.sum(mine, axis=1, keepdims=True)
-    fresh_count = jnp.sum(
-        jnp.where(iota((devices, fresh), 1) // slots == iota((devices, fresh), 0), count, 0.0),
-        axis=0,
-        keepdims=True,
-    )
-    fresh_valid = (iota((1, fresh), 1) % slots).astype(jnp.float32) < fresh_count
+    ahead_of = jnp.zeros((fresh, tok), jnp.float32)
+    for block in range(devices):
+        line = jnp.where(block < me, token_owner[block : block + 1, :], -1.0)
+        ahead_of = ahead_of + (line == row_owner).astype(jnp.float32)
+    position = (
+        start_at
+        + jnp.sum(ahead_of, axis=1, keepdims=True)
+        + (iota((fresh, 1), 0) % slots).astype(jnp.float32)
+    )
     half_size = HEAD // 2
     lane = iota((1, HEAD), 1)
     exponent = (lane % half_size).astype(jnp.float32) * (2.0 / HEAD)
@@ -443,9 +541,84 @@
     sine = jnp.sin(angle)
     sine = jnp.where(lane < half_size, -sine, sine)
 
-    for copy in locals_[4:]:
+    relay(0)
+    issue(2)
+    own_move = mover(me)
+    for b in range(outer):
+        locals_[chunks + b].wait()
+        acts[0, b] = dot32(own_move, raw[0, b]).astype(jnp.bfloat16)
+    gather(0)
+    relay(1)
+    issue(3)
+    gather(1)
+    relay(2)
+    issue(4)
+    for b in range(outer):
+        x_copy(b).wait_recv()
+        x_forward(b).start()
+    side_move = mover(mz * side + 1 - mx)
+    for b in range(outer):
+        x_forward(b).wait_recv()
+        acts[1, b] = dot32(side_move, raw[1, b]).astype(jnp.bfloat16)
+    for copy in locals_[:chunks]:
         copy.wait()
-    kv_local = width // HEAD
+
+    def product(i, j):
+        total = dot32(acts[i, 0], weights[j, 0])
+        for b in range(1, outer):
+            total = total + dot32(acts[i, b], weights[j, b])
+        return total
+
+    def multiply(j):
+        shipped[j] = product(1, j)
+        exchange(j).start()
+        return product(0, j)
+
+    def finish(j, own, low_parts):
+        exchange(j).wait_recv()
+        total = own + landed[j]
+        at = (j - 1) * HEAD
+        for piece in low_parts:
+            total = total + dot32(piece, upcat[:, at : at + HEAD])
+        if j <= kv_local:
+            total = total * cosine + pltpu.roll(total, half_size, 1) * sine
+        sent[j] = total.astype(jnp.bfloat16)
+        for o in range(1, devices):
+            part_copy(j, o).start()
+        mine_at = pl.ds(pl.multiple_of(me * slots, slots), slots)
+        got[j, mine_at, :] = sent[j, mine_at, :]
+
+    own_low = multiply(0)
+    own_1 = multiply(1)
+    gather(2)
+    own_2 = multiply(2)
+    exchange(0).wait_recv()
+    low_parts = halves(jnp.where(keep_low, own_low + landed[0], 0.0))
+    finish(1, own_1, low_parts)
+    relay(3)
+    finish(2, own_2, low_parts)
+    gather(3)
+    own_3 = multiply(3)
+    relay(4)
+    finish(3, own_3, low_parts)
+    gather(4)
+    own_4 = multiply(4)
+
+    mine = (token_owner[...] == me.astype(jnp.float32)).astype(jnp.float32)
+    context = jnp.sum(
+        jnp.where(iota((1, devices), 1) == me, context_ref[...].astype(jnp.float32), 0.0),
+        axis=1,
+        keepdims=True,
+    )
+    count = jnp.sum(mine, axis=1, keepdims=True)
+    fresh_count = jnp.sum(
+        jnp.where(iota((devices, fresh), 1) // slots == iota((devices, fresh), 0), count, 0.0),
+        axis=0,
+        keepdims=True,
+    )
+    fresh_valid = (iota((1, fresh), 1) % slots).astype(jnp.float32) < fresh_count
+    for copy in locals_[rest_at:]:
+        copy.wait()
     members = HEADS // KV_HEADS
     scale = HEAD ** (-0.5)
     query = query_ref[...].astype(jnp.float32)
@@ -466,22 +639,20 @@
             jnp.sum(heads * lastk_ref[:, cols].astype(jnp.float32), axis=1, keepdims=True) * scale
         )
 
-    def settle(k, carry):
+    def settle(j):
         for o in range(1, devices):
-            part_copy(k, o).wait_recv()
-        return carry
-
-    lax.fori_loop(0, devices, settle, 0)
+            part_arrival(j, o).wait_recv()
+
+    fresh_scores_of = []
+    for h in range(kv_local):
+        settle(1 + h)
+        fresh_scores_of.append(
+            jnp.where(fresh_valid, dot_rows(queries[h], got[1 + h]) * scale, -1e30)
+        )
+    finish(4, own_4, low_parts)
     for h in range(kv_local):
         cols = slice(h * HEAD, (h + 1) * HEAD)
-        key = got[0, :, cols].astype(jnp.float32)
-        value = got[0, :, width + h * HEAD : width + (h + 1) * HEAD].astype(jnp.float32)
-        for o in range(1, devices):
-            key = key + got[o, :, cols].astype(jnp.float32)
-            value = value + got[o, :, width + h * HEAD : width + (h + 1) * HEAD].astype(jnp.float32)
-        key = (key * cosine + pltpu.roll(key, half_size, 1) * sine).astype(jnp.bfloat16)
-        value = value.astype(jnp.bfloat16)
-        fresh_scores = jnp.where(fresh_valid, dot_rows(queries[h], key) * scale, -1e30)
+        fresh_scores = fresh_scores_of[h]
         top = jnp.maximum(
             jnp.maximum(
                 jnp.max(old_scores[h], axis=1, keepdims=True),
@@ -497,6 +668,8 @@
             + jnp.sum(fresh_weights, axis=1, keepdims=True)
             + last_weight
         )
+        settle(1 + kv_local + h)
+        value = got[1 + kv_local + h]
         mixed = dot32((old_weights / total).astype(jnp.bfloat16), oldv[:, cols])
         mixed = mixed + dot32((fresh_weights / total).astype(jnp.bfloat16), value)
         mixed = mixed + (last_weight / total).astype(jnp.bfloat16).astype(jnp.float32) * lastv_ref[
@@ -542,17 +715,40 @@
     )
     swap.start()
 
-    for k in range(1, devices):
-        x_copy(k).wait_send()
-        forward(k).wait_send()
-        mix_copy(k, me).wait_send()
-
-    def drain(k, carry):
-        for o in range(1, devices):
-            part_copy(k, o).wait_send()
-        return carry
-
-    lax.fori_loop(0, devices, drain, 0)
+    for b in range(outer):
+        x_copy(b).wait_send()
+        x_forward(b).wait_send()
+    for o in range(1, devices):
+        mix_copy(o, me).wait_send()
+    for j in range(chunks):
+        exchange(j).wait_send()
+        if j > 0:
+            for o in range(1, devices):
+                part_copy(j, o).wait_send()
+
+        @pl.when(mz < outer - 1)
+        def _():
+            z_first(j, True).wait_send()
+
+        @pl.when(mz > 0)
+        def _():
+            z_first(j, False).wait_send()
+
+        for t in range(1, outer):
+            for up in (True, False):
+                b = mz - t if up else mz + t
+
+                @pl.when(b >= 0 if up else b < outer)
+                def _():
+                    @pl.when(mz < outer - 1 if up else mz > 0)
+                    def _():
+                        z_relay(j, b, up).wait_send()
+
+                    y_copy(j, b).wait_send()
+                    if j == 0:
+                        q_copy(b, group, 0).wait_send()
+                        q_copy(b, 1 - group, 1).wait_send()
+
     swap.wait()
     out_ref[...] = (part[...] + other[...]).astype(jnp.bfloat16)
 
@@ -585,6 +781,9 @@
     slots = capacity * PAGE
     rows = request_adapter.shape[0]
     heads = step_query.shape[1] // HEAD
+    outer = devices // side
+    chunks = 1 + 2 * (width // HEAD)
+    fresh = devices * slots
     out_width = output_matrix.shape[1]
     bf16, f32 = jnp.bfloat16, jnp.float32
     whole = pl.BlockSpec(memory_space=pltpu.VMEM)
@@ -596,12 +795,15 @@
         in_specs=[far] * 4 + [whole] * 8 + [far] * 5,
         out_specs=whole,
         scratch_shapes=[
-            pltpu.VMEM((devices, tok, depth), bf16),
-            pltpu.VMEM((depth, 2 * width + low), bf16),
+            pltpu.VMEM((2, outer, tok, depth), bf16),
+            pltpu.VMEM((2, outer, tok, depth), bf16),
+            pltpu.VMEM((chunks, outer, depth, HEAD), bf16),
             pltpu.VMEM((low, 2 * width), bf16),
             pltpu.VMEM((devices, tok), f32),
-            pltpu.VMEM((devices, devices * slots, 2 * width), bf16),
-            pltpu.VMEM((devices, devices * slots, 2 * width), bf16),
+            pltpu.VMEM((chunks, fresh, HEAD), f32),
+            pltpu.VMEM((chunks, fresh, HEAD), f32),
+            pltpu.VMEM((chunks, fresh, HEAD), bf16),
+            pltpu.VMEM((chunks, fresh, HEAD), bf16),
             pltpu.VMEM(stored_keys.shape[1:], bf16),
             pltpu.VMEM(stored_values.shape[1:], bf16),
             pltpu.VMEM(output_matrix.shape, bf16),
@@ -610,13 +812,21 @@
             pltpu.VMEM((devices, heads, HEAD), f32),
             pltpu.VMEM((rows, out_width), f32),
             pltpu.VMEM((rows, out_width), f32),
-            dma((9,)),
-            dma((devices,)),
-            dma((devices,)),
-            dma((devices,)),
-            dma((devices,)),
-            dma((devices, devices)),
-            dma((devices, devices)),
+            dma((chunks + outer + 5,)),
+            dma((outer,)),
+            dma((outer,)),
+            dma((outer,)),
+            dma((outer,)),
+            dma((chunks, outer, 2)),
+            dma((chunks, outer)),
+            dma((chunks, outer)),
+            dma((chunks, outer)),
+            dma((outer, 2)),
+            dma((outer, 2)),
+            dma((chunks,)),
+            dma((chunks,)),
+            dma((chunks, devices)),
+            dma((chunks, devices)),
             dma((devices,)),
             dma((devices,)),
             dma,
@@ -657,13 +867,16 @@
     slots = slots_of(tok // PAGE, devices) * PAGE
     fits = (
         lax.axis_size("tp") == 2
+        and lax.axis_size("group") == 2
+        and devices >= 4
         and args[6].shape[0] == devices
         and devices % 2 == 0
         and devices <= 16
         and devices * slots == tok
         and tok <= 256
         and depth % 128 == 0
-        and width % HEAD == 0
+        and width == 2 * HEAD
+        and args[3].shape[1] == HEAD
         and slots % 16 == 0
     )
     if fits:

time: 114 us -> 97 us (0.85)
  Pallas kernels: 108 us -> 90.9 us
    pallas_call x1, Pallas kernels: 108 us -> 90.9 us  [fused(): pl.pallas_call(functools.partial(fused_kernel, devices, side, capacity),...]
where the time goes in v2:
time: 97 us; the launch traced here: 96.7 us
  Pallas kernels  90.9 us (94%)
  local copies, waits for them, and re-layouts  4.45 us (5%)
  other arithmetic  1.34 us (1%)
    pallas_call x1, Pallas kernels, fused(): pl.pallas_call(functools.partial(fused_kernel, devices, side, capacity),...  90.9 us
    unnamed x3, local copies, waits for them, and re-layouts  3.78 us

profile of v2, /device:TPU:0, one launch (start us, length us, event | category | flops | bytes accessed | tf_op | source)
XLA Modules:
  0.0 96.7 jit_solution(15467903407573988486)
XLA Ops:
  0.0 0.5 broadcast.3
  0.5 1.3 %reduce.3 = s32[512]{0:T(512)S(1)} reduce(s32[512,1]{0,1:T(1,128)} %param.24, s32[]{:T(128)} %broadcast.3), dimensions={1}, to_apply=%param.24.reduce_sub_computation.3 | reduce | bytes 4100 | tf_op args[7]
  1.9 0.7 reshape.10.owner_ref
  2.5 1.9 %copy.18.ado_hbm = bf16[2048,64]{1,0:T(8,128)(2,1)} copy(bf16[2048,64]{0,1:T(8,128)(2,1)} %param.32) | data formatting | bytes 524288 | tf_op args[15]
  4.5 90.9 %shard_map.163 = bf16[8,1024]{1,0:T(8,128)(2,1)} custom-call(bf16[256,8192]{1,0:T(8,128)(2,1)} %x_hbm.1, bf16[1024,256]{1,0:T(8,128)(2,1)} %wk_hbm.1, bf16[1024,256]{1,0:T(8,128)(2,1)} %wv_hbm.1, bf16[1024,128]{1,0:T(8,128)(2,1)} %ad_hbm.1, bf16[64,256]{1,0:T(8,128)(2,1)} %upk_ref.1, bf16[64,256]{1,0:T(8,128)(2,1)} %upv_ref.1, s32[1,8]{1,0:T(1,128)} %bitcast.7, ...), custom_call_target="tpu_custom_call" | custom-call | tf_op jit(solution)/shard_map/pallas_call | solution.py:792
  95.4 1.3 %copy.20 = bf16[8,1024]{1,0:T(8,128)(2,1)} copy(bf16[8,1024]{1,0:T(8,128)(2,1)} %shard_map.163) | data formatting | bytes 32768

commit v3 on v2

--- a/solution.py
+++ b/solution.py
@@ -489,6 +489,9 @@
     for copy in locals_:
         copy.start()
 
+    relay(0)
+    issue(2)
+
     pages = owner_ref.shape[1]
     spread = (iota((pages, tok), 1) // PAGE == iota((pages, tok), 0)).astype(jnp.bfloat16)
     token_owner[...] = dot32(owner_ref[...].astype(jnp.float32).astype(jnp.bfloat16), spread)
@@ -541,22 +544,20 @@
     sine = jnp.sin(angle)
     sine = jnp.where(lane < half_size, -sine, sine)
 
-    relay(0)
-    issue(2)
     own_move = mover(me)
+    side_move = mover(mz * side + 1 - mx)
+    relay(1)
+    issue(3)
     for b in range(outer):
         locals_[chunks + b].wait()
         acts[0, b] = dot32(own_move, raw[0, b]).astype(jnp.bfloat16)
-    gather(0)
-    relay(1)
-    issue(3)
-    gather(1)
     relay(2)
     issue(4)
+    gather(0)
+    gather(1)
     for b in range(outer):
         x_copy(b).wait_recv()
         x_forward(b).start()
-    side_move = mover(mz * side + 1 - mx)
     for b in range(outer):
         x_forward(b).wait_recv()
         acts[1, b] = dot32(side_move, raw[1, b]).astype(jnp.bfloat16)
@@ -590,19 +591,19 @@
 
     own_low = multiply(0)
     own_1 = multiply(1)
+    relay(3)
     gather(2)
     own_2 = multiply(2)
+    gather(3)
+    own_3 = multiply(3)
     exchange(0).wait_recv()
     low_parts = halves(jnp.where(keep_low, own_low + landed[0], 0.0))
     finish(1, own_1, low_parts)
-    relay(3)
-    finish(2, own_2, low_parts)
-    gather(3)
-    own_3 = multiply(3)
     relay(4)
-    finish(3, own_3, low_parts)
     gather(4)
     own_4 = multiply(4)
+    finish(2, own_2, low_parts)
+    finish(3, own_3, low_parts)
 
     mine = (token_owner[...] == me.astype(jnp.float32)).astype(jnp.float32)
     context = jnp.sum(
@@ -694,7 +695,7 @@
     everyone = jnp.concatenate(
         [mixes[:, h, :] for h in range(kv_local * members)], axis=1
     ).astype(jnp.bfloat16)
-    narrowed = dot32(everyone, ado[...])
+    narrowed = dot_rows(everyone, ado[...])
     row_of = jnp.sum(
         jnp.where(iota((devices, devices), 0) == iota((devices, devices), 1), adapters, 0.0),
         axis=1,
@@ -807,7 +808,7 @@
             pltpu.VMEM(stored_keys.shape[1:], bf16),
             pltpu.VMEM(stored_values.shape[1:], bf16),
             pltpu.VMEM(output_matrix.shape, bf16),
-            pltpu.VMEM(adapter_down_output.shape, bf16),
+            pltpu.VMEM(adapter_down_output.shape[::-1], bf16),
             pltpu.VMEM(adapter_up_output.shape, bf16),
             pltpu.VMEM((devices, heads, HEAD), f32),
             pltpu.VMEM((rows, out_width), f32),
@@ -851,7 +852,7 @@
         stored_keys[0],
         stored_values[0],
         output_matrix,
-        adapter_down_output,
+        adapter_down_output.T,
         adapter_up_output,
     )
 

time: 97 us -> 85 us (0.88)
  Pallas kernels: 90.9 us -> 80.9 us
  local copies, waits for them, and re-layouts: 4.45 us -> 2.5 us
    pallas_call x1, Pallas kernels: 90.9 us -> 80.9 us  [fused(): pl.pallas_call(functools.partial(fused_kernel, devices, side, capacity),...]
    unnamed x3 -> x2, local copies, waits for them, and re-layouts: 3.78 us -> 1.83 us
where the time goes in v3:
time: 85 us; the launch traced here: 84.7 us
  Pallas kernels  80.9 us (95%)
  local copies, waits for them, and re-layouts  2.5 us (3%)
  other arithmetic  1.34 us (2%)
    pallas_call x1, Pallas kernels, fused(): pl.pallas_call(functools.partial(fused_kernel, devices, side, capacity),...  80.9 us
    unnamed x2, local copies, waits for them, and re-layouts  1.83 us

profile of v3, /device:TPU:0, one launch (start us, length us, event | category | flops | bytes accessed | tf_op | source)
XLA Modules:
  0.0 84.7 jit_solution(12925331816526807770)
XLA Ops:
  0.0 0.5 broadcast.3
  0.5 1.3 %reduce.3 = s32[512]{0:T(512)S(1)} reduce(s32[512,1]{0,1:T(1,128)} %param.24, s32[]{:T(128)} %broadcast.3), dimensions={1}, to_apply=%param.24.reduce_sub_computation.3 | reduce | bytes 4100 | tf_op args[7]
  1.9 0.7 reshape.10.owner_ref
  2.5 80.9 %shard_map.163 = bf16[8,1024]{1,0:T(8,128)(2,1)} custom-call(bf16[256,8192]{1,0:T(8,128)(2,1)} %x_hbm.1, bf16[1024,256]{1,0:T(8,128)(2,1)} %wk_hbm.1, bf16[1024,256]{1,0:T(8,128)(2,1)} %wv_hbm.1, bf16[1024,128]{1,0:T(8,128)(2,1)} %ad_hbm.1, bf16[64,256]{1,0:T(8,128)(2,1)} %upk_ref.1, bf16[64,256]{1,0:T(8,128)(2,1)} %upv_ref.1, s32[1,8]{1,0:T(1,128)} %bitcast.9, ...), custom_call_target="tpu_custom_call" | custom-call | tf_op jit(solution)/shard_map/pallas_call | solution.py:793
  83.4 1.3 %copy.19 = bf16[8,1024]{1,0:T(8,128)(2,1)} copy(bf16[8,1024]{1,0:T(8,128)(2,1)} %shard_map.163) | data formatting | bytes 32768
